TPU v7x, 512 devices: a whole 4x4x16 slice. The times are simulated.
512 devices in a mesh: batch: 64 (over z_lo, y, core), space: 8 (over x, z_hi).
Axes of the slice: x: 4, y: 4, z: 16 (z_hi: 2, z_lo: 8; z = z_hi * 8 + z_lo), core: 2. Of those that a mesh axis runs over, the one named last changes fastest.
Arguments:
- acts: bfloat16 [64, 32, 64, 640], P('batch', 'space'), may hold values from -6 to 6
- conv_weight: bfloat16 [5760, 640], P('batch', 'space'), may hold values from -0.078125 to 0.078125
- conv_bias: float32 [640], replicated, may hold values from -4 to 4
- out_cotangent: bfloat16 [64, 32, 64, 640], P('batch', 'space'), may hold values from -6 to 6
- basis_in: bfloat16 [5760, 64], P('batch'), may hold values from -0.078125 to 0.078125
- basis_out: bfloat16 [640, 64], P('batch'), may hold values from -0.25 to 0.25
- query_ids: int32 [8], replicated, may hold values from 0 to 63
Outputs:
- activated: bfloat16 [64, 32, 64, 640], P('batch', 'space')
- basis_in_new: bfloat16 [5760, 64], P('batch')
- scores: float32 [8, 64], P(None, 'batch')
All inputs are finite; a program needn't handle non-finite values.
Results may differ from a plain program's by a relative error of at most 0.0031.
Values may be sent and summed in bfloat16 or wider, within the bound.
No kernel may reach another device: no remote copies, remote signals or barrier semaphores. Data moves between devices by JAX's collectives and lax.ppermute only.
A program may use at most 64 MiB of HBM per device.

v0:
```python
import math
import jax
import jax.numpy as jnp
from jax import lax
from jax.sharding import PartitionSpec as P

DAMPING = 0.1


def extended(value, sides, width):
    for axis, dim in sides:
        size, length = (lax.axis_size(axis), value.shape[dim])
        up = [(i, (i + 1) % size) for i in range(size - 1)]
        down = [(j, i) for i, j in up]
        last = lax.slice_in_dim(value, length - width, length, axis=dim)
        initial = lax.slice_in_dim(value, 0, width, axis=dim)
        before = lax.ppermute(last, axis, up)
        after = lax.ppermute(initial, axis, down)
        value = jnp.concatenate([before, value, after], axis=dim)
    return value


def add_columns(segment, operand):
    return jnp.dot(operand, segment, preferred_element_type=jnp.float32)


def add_with_norms(segment, operand):
    summed = add_columns(segment, operand)
    squares = jnp.sum(jnp.square(segment.astype(jnp.float32)), axis=0)
    return (summed, squares)


def contract_rows(left_side, right_side):
    return lax.dot_general(
        left_side, right_side, (((0,), (0,)), ((), ())), preferred_element_type=jnp.float32
    )


def per_device(acts, conv_weight, conv_bias, out_cotangent, basis_in, basis_out, query_ids):
    ex_local, band_rows, band_cols, channels = acts.shape
    padded = extended(acts, (("space", 1),), 1)
    padded = jnp.pad(padded, ((0, 0), (0, 0), (1, 1), (0, 0)))
    shifted = [
        padded[:, row_shift : row_shift + band_rows, col_shift : col_shift + band_cols, :]
        for row_shift in range(3)
        for col_shift in range(3)
    ]
    positions = ex_local * band_rows * band_cols
    patches = jnp.stack(shifted, axis=3).reshape(positions, 9 * channels)
    kernel_cols = lax.all_gather(conv_weight, "batch", axis=0, tiled=True)
    preact = jnp.dot(
        patches,
        lax.all_gather(kernel_cols, "space", axis=1, tiled=True),
        preferred_element_type=jnp.float32,
    )
    preact = preact + conv_bias
    sigmoid_pre = jax.nn.sigmoid(preact)
    activated = (preact * sigmoid_pre).astype(jnp.bfloat16).reshape(acts.shape)
    grad_pre = (
        out_cotangent.reshape(positions, channels).astype(jnp.float32)
        * sigmoid_pre
        * (1.0 + preact * (1.0 - sigmoid_pre))
    ).astype(jnp.bfloat16)
    basis_rank = basis_in.shape[1]
    probe_in = add_columns(lax.all_gather(basis_in, "batch", axis=0, tiled=True), patches).astype(
        jnp.bfloat16
    )
    probe_out = add_columns(
        lax.all_gather(basis_out, "batch", axis=0, tiled=True), grad_pre
    ).astype(jnp.bfloat16)
    term_in = contract_rows(patches, probe_in)
    term_out = contract_rows(grad_pre, probe_out)
    summed = lax.psum((term_in, term_out), "space")
    owned_in, owned_out = (
        lax.psum_scatter(summed[0], "batch", scatter_dimension=0, tiled=True),
        lax.psum_scatter(summed[1], "batch", scatter_dimension=0, tiled=True),
    )
    total_positions = positions * lax.axis_size("batch") * lax.axis_size("space")
    basis_in_new = (owned_in / total_positions).astype(jnp.bfloat16)
    basis_out_new = (owned_out / total_positions).astype(jnp.bfloat16)
    raw_in, square_in = add_with_norms(
        lax.all_gather(basis_in_new, "batch", axis=0, tiled=True), patches
    )
    raw_out, square_out = add_with_norms(
        lax.all_gather(basis_out_new, "batch", axis=0, tiled=True), grad_pre
    )
    scale_in = jnp.sqrt(square_in)
    scale_out = jnp.sqrt(square_out)
    feat_in = (
        (raw_in / scale_in)
        .astype(jnp.bfloat16)
        .reshape(ex_local, band_rows * band_cols, basis_rank)
    )
    feat_out = (
        (raw_out / scale_out)
        .astype(jnp.bfloat16)
        .reshape(ex_local, band_rows * band_cols, basis_rank)
    )
    height = band_rows * lax.axis_size("space")
    projected = (
        jnp.einsum("epi,epj->eij", feat_out, feat_in, preferred_element_type=jnp.float32) / height
    )
    projected = lax.psum(projected, "space")
    scaled = projected / (scale_out[:, None] * scale_in[None, :] + DAMPING)
    all_projs = lax.all_gather(projected, "batch", axis=0, tiled=True)
    queries = jnp.take(all_projs, query_ids, axis=0)
    scores = jnp.einsum("qij,eij->qe", queries, scaled, precision=lax.Precision.HIGHEST) / (
        basis_rank * math.sqrt(basis_rank)
    )
    return (activated, basis_in_new, scores)


def solution(mesh):
    return jax.shard_map(
        per_device,
        mesh=mesh,
        in_specs=(
            P("batch", "space", None, None),
            P("batch", "space"),
            P(),
            P("batch", "space", None, None),
            P("batch", None),
            P("batch", None),
            P(),
        ),
        out_specs=(P("batch", "space", None, None), P("batch", None), P(None, "batch")),
        check_vma=False,
    )
```

profile of v0, /device:TPU:1, one launch (start us, length us, event | category | flops | bytes accessed | tf_op | source)
XLA Modules:
  0.0 1847.2 jit_solution(3337683036946885710)
XLA Ops:
  7.2 132.7 %all-gather = bf16[64,90,80]{1,2,0:T(8,128)(2,1)S(1)} all-gather(bf16[1,90,80]{1,2,0:T(8,128)(2,1)} %bitcast.90), channel_id=1, replica_groups=mesh['batch'=64,'space'=8] {'batch'}, dimensions={0}, use_global_device_ids=true | all-gather | bytes 936000 | tf_op jit(solution)/shard_map/all_gather | solution.py:50
  140.3 2.8 reshape.103
  143.2 8.0 collective-permute-start
  151.2 1.3 collective-permute-start.1
  152.5 167.6 %all-gather.1 = bf16[64,90,64]{1,2,0:T(8,128)(2,1)S(1)} all-gather(bf16[1,90,64]{1,2,0:T(8,128)(2,1)S(1)} %bitcast.91), channel_id=1, replica_groups=mesh['batch'=64,'space'=8] {'batch'}, dimensions={0}, use_global_device_ids=true | all-gather | bytes 748800 | tf_op jit(solution)/shard_map/all_gather | solution.py:65
  320.1 165.3 %all-gather.2 = bf16[64,10,64]{2,1,0:T(8,128)(2,1)S(1)} all-gather(bf16[1,10,64]{2,1,0:T(8,128)(2,1)S(1)} %bitcast.92), channel_id=1, replica_groups=mesh['batch'=64,'space'=8] {'batch'}, dimensions={0}, use_global_device_ids=true | all-gather | bytes 83200 | tf_op jit(solution)/shard_map/all_gather | solution.py:69
  486.2 2.4 reshape.105
  490.9 2.0 copy.14
  493.7 4.5 fusion.3
  498.3 6.4 fusion.11
  504.7 1.3 fusion.2
  506.1 1.3 dynamic-slice
  508.6 821.8 %all-reduce.7.cloned.1.call-done = (f32[5760,64]{0,1:T(8,128)}, f32[640,64]{1,0:T(8,128)}) async-done(((f32[5760,64]{0,1:T(8,128)}, f32[640,64]{1,0:T(8,128)}), (f32[5760,64]{0,1:T(8,128)}, f32[640,64]{1,0:T(8,128)})) %all-reduce.7.cloned.1.call-update) | async-done | bytes 1638416
  1332.0 66.9 %all-reduce.4 = (f32[90,64]{0,1:T(8,128)S(1)}, f32[10,64]{1,0:T(8,128)S(1)}) all-reduce(f32[90,64]{0,1:T(8,128)S(1)} %constant_dynamic-slice_fusion.1, f32[10,64]{1,0:T(8,128)S(1)} %constant_dynamic-slice_fusion), channel_id=1, replica_groups=mesh['batch'=64,'space'=8] {'space'}, use_global_device_ids=true, to_apply=%region_0.1 | all-reduce | flops 6400 | bytes 51200 | tf_op jit(solution)/shard_map/psum | solution.py:73
  1398.9 130.7 %all-gather.4 = bf16[64,90,64]{1,2,0:T(8,128)(2,1)S(1)} all-gather(bf16[1,90,64]{1,2,0:T(8,128)(2,1)S(1)} %fusion.45), channel_id=1, replica_groups=mesh['batch'=64,'space'=8] {'batch'}, dimensions={0}, use_global_device_ids=true | all-gather | bytes 748800 | tf_op jit(solution)/shard_map/all_gather | solution.py:82
  1529.6 1.6 copy.17
  1531.2 3.1 reshape.111
  1534.4 1.4 multiply_reduce_fusion
  1535.8 114.8 %all-gather.3 = bf16[64,10,64]{2,1,0:T(8,128)(2,1)S(1)} all-gather(bf16[1,10,64]{2,1,0:T(8,128)(2,1)S(1)} %fusion.29), channel_id=1, replica_groups=mesh['batch'=64,'space'=8] {'batch'}, dimensions={0}, use_global_device_ids=true | all-gather | bytes 83200 | tf_op jit(solution)/shard_map/all_gather | solution.py:85
  1653.5 2.3 fusion.6
  1655.7 60.8 %psum.23 = f32[1,64,64]{2,1,0:T(8,128)} all-reduce(f32[1,64,64]{2,1,0:T(8,128)S(1)} %fusion.6), channel_id=1, replica_groups=mesh['batch'=64,'space'=8] {'space'}, use_global_device_ids=true, to_apply=%region_6.7 | all-reduce | flops 4096 | bytes 32768 | tf_op jit(solution)/shard_map/psum | solution.py:103
  1718.1 119.1 %all-gather.10.cloned.1.call-done = f32[64,64,64]{2,1,0:T(8,128)} async-done(((f32[1,64,64]{2,1,0:T(8,128)}), f32[64,64,64]{2,1,0:T(8,128)}) %all-gather.10.cloned.1.call-update) | async-done | bytes 1048592 | tf_op jit(solution)/shard_map/all_gather | solution.py:105
  1837.2 2.2 gather_fusion
  1839.5 1.2 fusion.8
  (55 shorter events, 10.5 us)
Async XLA Ops:
  7.2 491.1 %all-gather.8.cloned.1.call-start = ((), (), s32[]{:S(2)}) async-start(), calls=%async_computation | async-start | bytes 8294400 | tf_op jit(solution)/shard_map/all_gather | solution.py:53
  139.9 3.2 copy-start
  139.9 12.6 copy-start.4
  140.0 180.1 %copy-start.5 = (bf16[10,64]{1,0:T(8,128)(2,1)S(1)}, bf16[10,64]{1,0:T(8,128)(2,1)}, u32[]{:S(2)}) copy-start(bf16[10,64]{1,0:T(8,128)(2,1)} %param.12) | copy-start | bytes 3844
  143.1 1187.3 %all-reduce.7.cloned.1.call-start = ((), (), s32[]{:S(2)}) async-start(), calls=%async_computation.2 | async-start | bytes 3604480
  143.2 345.4 %collective-permute-start = (bf16[1,1,64,640]{3,2,1,0:T(8,128)(2,1)S(1)}, bf16[1,1,64,640]{3,2,1,0:T(8,128)(2,1)S(1)}, u32[]{:S(2)}, u32[]{:S(2)}) collective-permute-start(bf16[1,1,64,640]{3,2,1,0:T(8,128)(2,1)S(1)} %get-tuple-element.9), channel_id=1, source_target_pairs={{0,1},{1,2},{2,3},{3,4},{4,5},{5,6},{6,7},{8,9},{9,10},{10,11},{11... | collective-permute-start | bytes 245768 | tf_op jit(solution)/shard_map/ppermute | solution.py:17
  151.2 337.4 %collective-permute-start.1 = (bf16[1,1,64,640]{3,2,1,0:T(8,128)(2,1)S(1)}, bf16[1,1,64,640]{3,2,1,0:T(8,128)(2,1)S(1)}, u32[]{:S(2)}, u32[]{:S(2)}) collective-permute-start(bf16[1,1,64,640]{3,2,1,0:T(8,128)(2,1)S(1)} %get-tuple-element.10), channel_id=1, source_target_pairs={{1,0},{2,1},{3,2},{4,3},{5,4},{6,5},{7,6},{9,8},{10,9},{11,10},{12... | collective-permute-start | bytes 245768 | tf_op jit(solution)/shard_map/ppermute | solution.py:18
  488.6 0.6 copy-start.1
  493.7 4.6 copy-start.6
  506.0 1331.2 %all-gather.10.cloned.1.call-start = ((), (), s32[]{:S(2)}) async-start(), calls=%async_computation.1 | async-start | bytes 2129920 | tf_op jit(solution)/shard_map/all_gather | solution.py:105
  1398.9 136.8 %copy-start.2 = (f32[90,64]{0,1:T(8,128)}, f32[90,64]{0,1:T(8,128)S(1)}, u32[]{:S(2)}) copy-start(f32[90,64]{0,1:T(8,128)S(1)} %get-tuple-element.5) | copy-start | bytes 69124
  1534.4 182.2 %copy-start.7 = (s32[8]{0:T(128)S(1)}, s32[8]{0:T(128)}, u32[]{:S(2)}) copy-start(s32[8]{0:T(128)} %param.13) | copy-start | bytes 100
  1651.3 65.3 %copy-start.3 = (f32[90,64]{0,1:T(8,128)S(1)}, f32[90,64]{0,1:T(8,128)}, u32[]{:S(2)}) copy-start(f32[90,64]{0,1:T(8,128)} %copy-done.2) | copy-start | bytes 69124
Sparse Core Ops, SparseCore 0:
  143.2 265.6 all-gather.7
  506.1 824.2 all-reduce.6
  1716.7 120.4 all-gather.9
where the time goes:
time: 1850 us
  waiting for transfers between devices  941 us (51%)
  blocking collectives  839 us (45%)
  local copies, waits for them, and re-layouts  20.8 us (1%)
    unnamed x4, waiting for transfers between devices  822 us
    all_gather x1, blocking collectives, per_device(): lax.all_gather(basis_in, 'batch', axis=0, tiled=True)  168 us
    all_gather x1, blocking collectives, per_device(): lax.all_gather(basis_out, 'batch', axis=0, tiled=True)  165 us
    all_gather x1, blocking collectives, per_device(): kernel_cols = lax.all_gather(conv_weight, 'batch', axis=0, tiled=True)  133 us
    all_gather x1, blocking collectives, per_device(): lax.all_gather(basis_in_new, 'batch', axis=0, tiled=True)  131 us
    all_gather x1, waiting for transfers between devices, per_device(): all_projs = lax.all_gather(projected, 'batch', axis=0, tiled=True)  119 us
    all_gather x1, blocking collectives, per_device(): lax.all_gather(basis_out_new, 'batch', axis=0, tiled=True)  115 us
    psum x1, blocking collectives, per_device(): summed = lax.psum((term_in, term_out), 'space')  66.9 us
  transfers between devices with their start and end apart: 5, of which 2 were waited for; matrix products, arithmetic and copies ran while one was open for 1% of the time, Pallas kernels for 0%

commit v1 on v0

--- a/solution.py
+++ b/solution.py
@@ -62,9 +62,12 @@
         * (1.0 + preact * (1.0 - sigmoid_pre))
     ).astype(jnp.bfloat16)
     basis_rank = basis_in.shape[1]
-    probe_in = add_columns(lax.all_gather(basis_in, "batch", axis=0, tiled=True), patches).astype(
-        jnp.bfloat16
-    )
+    probe_in = add_columns(
+        jnp.concatenate(
+            lax.all_to_all(jnp.stack([basis_in] * lax.axis_size("batch")), "batch", 0, 0), axis=0
+        ),
+        patches,
+    ).astype(jnp.bfloat16)
     probe_out = add_columns(
         lax.all_gather(basis_out, "batch", axis=0, tiled=True), grad_pre
     ).astype(jnp.bfloat16)

time: 1850 us -> 1810 us (0.978)
  blocking collectives: 839 us -> 671 us
  waiting for transfers between devices: 941 us -> 1060 us
    all_gather x1 -> x0, blocking collectives: 168 us -> none  [per_device(): lax.all_gather(basis_in, 'batch', axis=0, tiled=True)]
    all_gather x1, waiting for transfers between devices: 0.01 us -> 93.8 us  [per_device(): lax.all_gather(kernel_cols, 'space', axis=1, tiled=True)]
    unnamed x4, waiting for transfers between devices: 822 us -> 849 us
  transfers between devices with their start and end apart: 5 -> 6, of which waited for: 2 -> 3; matrix products, arithmetic and copies ran while one was open for 1% -> 1% of each run, Pallas kernels for 0% -> 0%
where the time goes in v1:
time: 1810 us
  waiting for transfers between devices  1060 us (59%)
  blocking collectives  671 us (37%)
  local copies, waits for them, and re-layouts  24.6 us (1%)
    unnamed x4, waiting for transfers between devices  849 us
    all_gather x1, blocking collectives, per_device(): lax.all_gather(basis_out, 'batch', axis=0, tiled=True)  167 us
    all_gather x1, blocking collectives, per_device(): kernel_cols = lax.all_gather(conv_weight, 'batch', axis=0, tiled=True)  131 us
    all_gather x1, blocking collectives, per_device(): lax.all_gather(basis_in_new, 'batch', axis=0, tiled=True)  131 us
    all_gather x1, waiting for transfers between devices, per_device(): all_projs = lax.all_gather(projected, 'batch', axis=0, tiled=True)  119 us
    all_gather x1, blocking collectives, per_device(): lax.all_gather(basis_out_new, 'batch', axis=0, tiled=True)  115 us
    all_gather x1, waiting for transfers between devices, per_device(): lax.all_gather(kernel_cols, 'space', axis=1, tiled=True)  93.8 us
    psum x1, blocking collectives, per_device(): summed = lax.psum((term_in, term_out), 'space')  66.9 us
  transfers between devices with their start and end apart: 6, of which 3 were waited for; matrix products, arithmetic and copies ran while one was open for 1% of the time, Pallas kernels for 0%

profile of v1, /device:TPU:1, one launch (start us, length us, event | category | flops | bytes accessed | tf_op | source)
XLA Modules:
  0.0 1808.7 jit_solution(14759491890769303178)
XLA Ops:
  7.2 130.9 %all-gather = bf16[64,90,80]{1,2,0:T(8,128)(2,1)S(1)} all-gather(bf16[1,90,80]{1,2,0:T(8,128)(2,1)} %bitcast.89), channel_id=1, replica_groups=mesh['batch'=64,'space'=8] {'batch'}, dimensions={0}, use_global_device_ids=true | all-gather | bytes 936000 | tf_op jit(solution)/shard_map/all_gather | solution.py:50
  138.5 2.8 reshape.109
  141.2 1.3 stack.32
  142.6 5.1 all-to-all-start
  147.7 7.9 collective-permute-start
  157.0 167.4 %all-gather.1 = bf16[64,10,64]{2,1,0:T(8,128)(2,1)S(1)} all-gather(bf16[1,10,64]{2,1,0:T(8,128)(2,1)S(1)} %bitcast.90), channel_id=1, replica_groups=mesh['batch'=64,'space'=8] {'batch'}, dimensions={0}, use_global_device_ids=true | all-gather | bytes 83200 | tf_op jit(solution)/shard_map/all_gather | solution.py:72
  325.3 2.0 copy.14
  328.1 3.0 copy.16
  331.1 3.2 reshape.96
  334.3 4.6 fusion.3
  338.8 93.8 %all-gather.7.cloned.1.call-done = bf16[5760,640]{0,1:T(8,128)(2,1)} async-done(((bf16[5760,80]{0,1:T(8,128)(2,1)}), bf16[5760,640]{0,1:T(8,128)(2,1)}) %all-gather.7.cloned.1.call-update) | async-done | bytes 7372816 | tf_op jit(solution)/shard_map/all_gather | solution.py:53
  432.7 6.4 fusion.11
  439.0 1.3 fusion.2
  443.0 848.9 %all-reduce.7.cloned.1.call-done = (f32[5760,64]{0,1:T(8,128)}, f32[640,64]{1,0:T(8,128)}) async-done(((f32[5760,64]{0,1:T(8,128)}, f32[640,64]{1,0:T(8,128)}), (f32[5760,64]{0,1:T(8,128)}, f32[640,64]{1,0:T(8,128)})) %all-reduce.7.cloned.1.call-update) | async-done | bytes 1638416
  1293.6 66.9 %all-reduce.4 = (f32[90,64]{0,1:T(8,128)S(1)}, f32[10,64]{1,0:T(8,128)S(1)}) all-reduce(f32[90,64]{0,1:T(8,128)S(1)} %constant_dynamic-slice_fusion.1, f32[10,64]{1,0:T(8,128)S(1)} %constant_dynamic-slice_fusion), channel_id=1, replica_groups=mesh['batch'=64,'space'=8] {'space'}, use_global_device_ids=true, to_apply=%region_0.1 | all-reduce | flops 6400 | bytes 51200 | tf_op jit(solution)/shard_map/psum | solution.py:76
  1360.5 130.6 %all-gather.3 = bf16[64,90,64]{1,2,0:T(8,128)(2,1)S(1)} all-gather(bf16[1,90,64]{1,2,0:T(8,128)(2,1)S(1)} %fusion.45), channel_id=1, replica_groups=mesh['batch'=64,'space'=8] {'batch'}, dimensions={0}, use_global_device_ids=true | all-gather | bytes 748800 | tf_op jit(solution)/shard_map/all_gather | solution.py:85
  1491.1 1.7 copy.17
  1492.7 3.1 reshape.115
  1495.8 1.4 multiply_reduce_fusion
  1497.3 114.8 %all-gather.2 = bf16[64,10,64]{2,1,0:T(8,128)(2,1)S(1)} all-gather(bf16[1,10,64]{2,1,0:T(8,128)(2,1)S(1)} %fusion.29), channel_id=1, replica_groups=mesh['batch'=64,'space'=8] {'batch'}, dimensions={0}, use_global_device_ids=true | all-gather | bytes 83200 | tf_op jit(solution)/shard_map/all_gather | solution.py:88
  1615.0 2.3 fusion.6
  1617.2 60.8 %psum.23 = f32[1,64,64]{2,1,0:T(8,128)} all-reduce(f32[1,64,64]{2,1,0:T(8,128)S(1)} %fusion.6), channel_id=1, replica_groups=mesh['batch'=64,'space'=8] {'space'}, use_global_device_ids=true, to_apply=%region_6.7 | all-reduce | flops 4096 | bytes 32768 | tf_op jit(solution)/shard_map/psum | solution.py:106
  1679.6 119.1 %all-gather.9.cloned.1.call-done = f32[64,64,64]{2,1,0:T(8,128)} async-done(((f32[1,64,64]{2,1,0:T(8,128)}), f32[64,64,64]{2,1,0:T(8,128)}) %all-gather.9.cloned.1.call-update) | async-done | bytes 1048592 | tf_op jit(solution)/shard_map/all_gather | solution.py:108
  1798.7 2.2 gather_fusion
  (55 shorter events, 12.1 us)
Async XLA Ops:
  7.2 425.5 %all-gather.7.cloned.1.call-start = ((), (), s32[]{:S(2)}) async-start(), calls=%async_computation.1 | async-start | bytes 8294400 | tf_op jit(solution)/shard_map/all_gather | solution.py:53
  138.1 3.2 copy-start.3
  138.4 9.3 copy-start
  138.4 18.5 %copy-start.4 = (bf16[10,64]{1,0:T(8,128)(2,1)S(1)}, bf16[10,64]{1,0:T(8,128)(2,1)}, u32[]{:S(2)}) copy-start(bf16[10,64]{1,0:T(8,128)(2,1)} %param.12) | copy-start | bytes 3844
  142.6 185.6 %all-to-all-start = ((bf16[64,90,64]{1,2,0:T(8,128)(2,1)}), bf16[64,90,64]{1,2,0:T(8,128)(2,1)}, u32[]{:S(2)}, u32[]{:S(2)}) async-start(bf16[64,90,64]{1,2,0:T(8,128)(2,1)} %stack.32), calls=%async_computation | async-start | bytes 2097152 | tf_op jit(solution)/shard_map/all_to_all | solution.py:67
  147.6 1144.3 %all-reduce.7.cloned.1.call-start = ((), (), s32[]{:S(2)}) async-start(), calls=%async_computation.3 | async-start | bytes 3604480
  147.7 176.7 %collective-permute-start = (bf16[1,1,64,640]{3,2,1,0:T(8,128)(2,1)S(1)}, bf16[1,1,64,640]{3,2,1,0:T(8,128)(2,1)S(1)}, u32[]{:S(2)}, u32[]{:S(2)}) collective-permute-start(bf16[1,1,64,640]{3,2,1,0:T(8,128)(2,1)S(1)} %get-tuple-element.9), channel_id=1, source_target_pairs={{0,1},{1,2},{2,3},{3,4},{4,5},{5,6},{6,7},{8,9},{9,10},{10,11},{11... | collective-permute-start | bytes 245768 | tf_op jit(solution)/shard_map/ppermute | solution.py:17
  155.7 168.8 %collective-permute-start.1 = (bf16[1,1,64,640]{3,2,1,0:T(8,128)(2,1)S(1)}, bf16[1,1,64,640]{3,2,1,0:T(8,128)(2,1)S(1)}, u32[]{:S(2)}, u32[]{:S(2)}) collective-permute-start(bf16[1,1,64,640]{3,2,1,0:T(8,128)(2,1)S(1)} %get-tuple-element.10), channel_id=1, source_target_pairs={{1,0},{2,1},{3,2},{4,3},{5,4},{6,5},{7,6},{9,8},{10,9},{11,10},{12... | collective-permute-start | bytes 245768 | tf_op jit(solution)/shard_map/ppermute | solution.py:18
  334.3 98.4 %copy-start.5 = (f32[640]{0:T(1024)S(1)}, f32[640]{0:T(1024)}, u32[]{:S(2)}) copy-start(f32[640]{0:T(1024)} %param.9) | copy-start | bytes 7684
  440.4 1358.3 %all-gather.9.cloned.1.call-start = ((), (), s32[]{:S(2)}) async-start(), calls=%async_computation.2 | async-start | bytes 2129920 | tf_op jit(solution)/shard_map/all_gather | solution.py:108
  1360.5 136.8 %copy-start.1 = (f32[90,64]{0,1:T(8,128)}, f32[90,64]{0,1:T(8,128)S(1)}, u32[]{:S(2)}) copy-start(f32[90,64]{0,1:T(8,128)S(1)} %get-tuple-element.5) | copy-start | bytes 69124
  1495.8 182.2 %copy-start.6 = (s32[8]{0:T(128)S(1)}, s32[8]{0:T(128)}, u32[]{:S(2)}) copy-start(s32[8]{0:T(128)} %param.13) | copy-start | bytes 100
  1612.8 65.3 %copy-start.2 = (f32[90,64]{0,1:T(8,128)S(1)}, f32[90,64]{0,1:T(8,128)}, u32[]{:S(2)}) copy-start(f32[90,64]{0,1:T(8,128)} %copy-done.1) | copy-start | bytes 69124
Sparse Core Ops, SparseCore 0:
  141.4 291.2 all-gather.6
  440.5 851.3 all-reduce.6
  1678.2 120.4 all-gather.8
